TPU v7x, 32 devices: a whole 2x2x4 slice. The times are simulated.
32 devices in a mesh: dp: 8 (over z, core), mp: 4 (over y, x).
Axes of the slice: x: 2, y: 2, z: 4, core: 2. Of those that a mesh axis runs over, the one named last changes fastest.
Arguments:
- inputs: bfloat16 [1024, 32768], P('dp', 'mp'), may hold values from -6 to 6
- cotangent: bfloat16 [1024, 32768], P('dp', 'mp'), may hold values from -6 to 6
- first_weight: bfloat16 [128, 2, 256, 256], P('mp', None, 'dp'), may hold values from -0.25 to 0.25
- second_weight: bfloat16 [128, 2, 256, 256], P('mp', None, 'dp'), may hold values from -0.25 to 0.25
- orders: int32 [2, 256], replicated, may hold values from 0 to 255, each once within a row
Outputs:
- input_grad: bfloat16 [1024, 32768], P('dp', 'mp')
- first_grad: float32 [128, 2, 256, 256], P('mp', None, 'dp')
- second_grad: float32 [128, 2, 256, 256], P('mp', None, 'dp')
Inputs may be any that keep to these rules, and one draw needn't show every extreme that they name: Each of the two rows of orders is a permutation of 0 to 255.
All inputs are finite; a program needn't handle non-finite values.
Results may differ from a plain program's by a relative error of at most 0.018.
Values may be sent and summed in bfloat16 or wider, within the bound.
A program may use at most 128 MiB of HBM per device.

v0:
```python
import math
import jax
import jax.numpy as jnp
from jax import lax
from jax.sharding import PartitionSpec as P

B = 256


def partner(value, axis, bit):
    mask = 2**bit
    pairs = [(source, source ^ mask) for source in range(lax.axis_size(axis))]
    return lax.ppermute(value, axis, pairs)


def gelu_tanh(argument):
    return jax.nn.gelu(argument, approximate=True)


def inverse_order(order):
    length = order.shape[0]
    positions = jnp.arange(length, dtype=jnp.int32)
    matches = order[None, :] == positions[:, None]
    return jnp.sum(jnp.where(matches, positions[None, :], 0), axis=1)


def contract(left, right):
    return jnp.einsum("tnk,nkj->tnj", left, right, preferred_element_type=jnp.float32)


def contract_back(left, right):
    return jnp.einsum("tnj,nkj->tnk", left, right, preferred_element_type=jnp.float32)


def outer_sum(left, right):
    return jnp.einsum("tnk,tnj->nkj", left, right, preferred_element_type=jnp.float32)


def shards(inputs, cotangent, first_weight, second_weight, orders):
    tok_rows = inputs.shape[0]
    feature_width = inputs.shape[1]
    local_blocks = feature_width // B
    bit_top = lax.axis_size("mp").bit_length() - 2
    bit_next = bit_top - 1
    grad_scale = 1.0 / math.sqrt(tok_rows * lax.axis_size("dp"))
    order_first = orders[0]
    order_second = orders[1]
    inverse_first = inverse_order(order_first)
    inverse_second = inverse_order(order_second)
    first_full = lax.all_gather(first_weight, "dp", axis=2, tiled=True)
    own_first = first_full[:, 0]
    cross_first = jnp.take(first_full[:, 1], inverse_first, axis=1)
    blocks_in = inputs.reshape(tok_rows, local_blocks, B)
    partner_in = partner(inputs, "mp", bit_top).reshape(tok_rows, local_blocks, B)
    pre_act = contract(blocks_in, own_first) + contract(partner_in, cross_first)
    saved_pre = pre_act.astype(jnp.bfloat16)
    activated = gelu_tanh(pre_act).astype(jnp.bfloat16)
    blocks_cot = cotangent.reshape(tok_rows, local_blocks, B)
    moved_rows = partner(second_weight[:, 1:], "mp", bit_next)
    held_rows = jnp.concatenate([second_weight[:, :1], moved_rows], axis=1)
    second_full = lax.all_gather(held_rows, "dp", axis=2, tiled=True)
    own_second = second_full[:, 0]
    cross_second = jnp.take(second_full[:, 1], inverse_second, axis=1)
    cot_partner = partner(blocks_cot, "mp", bit_next)
    cross_two = contract_back(cot_partner, cross_second).astype(jnp.bfloat16)
    grad_cross = jnp.take(outer_sum(activated, cot_partner), order_second, axis=1)
    act_grad = contract_back(blocks_cot, own_second) + cross_two.astype(jnp.float32)
    pullback = jax.vjp(gelu_tanh, saved_pre.astype(jnp.float32))[1]
    pre_grad = pullback(act_grad)[0].astype(jnp.bfloat16)
    second_term = jnp.stack([outer_sum(activated, blocks_cot), grad_cross], axis=1) * grad_scale
    product_one = contract_back(pre_grad, cross_first).astype(jnp.bfloat16)
    cross_one = partner(product_one, "mp", bit_top)
    input_grad = (contract_back(pre_grad, own_first) + cross_one.astype(jnp.float32)).astype(
        jnp.bfloat16
    )
    input_grad = input_grad.reshape(tok_rows, feature_width)
    first_cross = jnp.take(outer_sum(partner_in, pre_grad), order_first, axis=1)
    first_term = jnp.stack([outer_sum(blocks_in, pre_grad), first_cross], axis=1) * grad_scale
    first_sum, second_sum = (
        lax.psum_scatter(
            first_term.astype(jnp.bfloat16), "dp", scatter_dimension=2, tiled=True
        ).astype(jnp.float32),
        lax.psum_scatter(
            second_term.astype(jnp.bfloat16), "dp", scatter_dimension=2, tiled=True
        ).astype(jnp.float32),
    )
    returned = partner(second_sum[:, 1:].astype(jnp.bfloat16), "mp", bit_next).astype(jnp.float32)
    second_sum = jnp.concatenate([second_sum[:, :1], returned], axis=1)
    return (input_grad, first_sum, second_sum)


def solution(mesh):
    in_specs = (
        P("dp", "mp"),
        P("dp", "mp"),
        P("mp", None, "dp", None),
        P("mp", None, "dp", None),
        P(),
    )
    out_specs = (P("dp", "mp"), P("mp", None, "dp", None), P("mp", None, "dp", None))
    return jax.shard_map(shards, mesh=mesh, in_specs=in_specs, out_specs=out_specs, check_vma=False)
```

profile of v0, /device:TPU:0, one launch (start us, length us, event | category | flops | bytes accessed | tf_op | source)
XLA Modules:
  0.0 375.4 jit_solution(8754357749359150172)
XLA Ops:
  7.2 2.9 copy.92
  11.5 3.0 collective-permute-start
  14.5 11.9 %collective-permute-done = bf16[32,1,32,256]{3,2,0,1:T(8,128)(2,1)S(1)} collective-permute-done((bf16[32,1,32,256]{3,2,0,1:T(8,128)(2,1)S(1)}, bf16[32,1,32,256]{3,2,0,1:T(8,128)(2,1)S(1)}, u32[]{:S(2)}, u32[]{:S(2)}) %collective-permute-start) | collective-permute-done | bytes 524320 | tf_op jit(solution)/shard_map/ppermute | solution.py:13
  27.7 2.4 copy.96
  30.1 1.8 collective-permute-start.2
  31.9 3.3 copy.87
  35.2 2.9 copy.90
  38.1 1.5 collective-permute-start.1
  39.8 55.3 %all-gather.5.cloned.1.call-done = bf16[32,2,256,256]{3,0,1,2:T(8,128)(2,1)} async-done(((bf16[32,2,32,256]{3,0,1,2:T(8,128)(2,1)}), bf16[32,2,256,256]{3,0,1,2:T(8,128)(2,1)}) %all-gather.5.cloned.1.call-update) | async-done | bytes 8388624 | tf_op jit(solution)/shard_map/all_gather | solution.py:50
  95.1 6.0 %slice_bitcast_fusion = (bf16[32,256,256]{2,0,1:T(8,128)(2,1)}, bf16[32,1,256,256]{3,0,1,2:T(8,128)(2,1)}) fusion(bf16[32,2,256,256]{3,0,1,2:T(8,128)(2,1)} %all-gather.5.cloned.1.call-done), kind=kLoop, calls=%fused_computation.32 | loop fusion | bytes 16777216 | tf_op jit(solution)/shard_map/squeeze | solution.py:52
  101.0 7.8 %copy.130 = bf16[32,1,256,256]{2,3,0,1:T(8,128)(2,1)} copy(bf16[32,1,256,256]{3,0,1,2:T(8,128)(2,1)} %get-tuple-element.18) | data formatting | bytes 8388608
  108.8 5.0 %gather_fusion.1 = bf16[256,32,256]{2,1,0:T(8,128)(2,1)} fusion(bf16[32,256,256]{2,0,1:T(8,128)(2,1)} %get-tuple-element.17, s32[1024]{0:T(1024)S(1)} %pad_clamp_fusion.2), kind=kCustom, calls=%fused_computation.2.clone | custom fusion | bytes 8389632 | tf_op jit(solution)/shard_map/jit(_take)/gather | solution.py:52
  113.8 3.4 select_bitcast_fusion.2
  119.4 6.9 %fusion.32 = f32[32,256,128]{2,1,0:T(8,128)S(1)} fusion(f32[32,256,128]{2,1,0:T(8,128)S(1)} %fusion.23, bf16[128,32,256]{0,2,1:T(8,128)(2,1)} %bitcast.10, bf16[32,256,256]{2,0,1:T(8,128)(2,1)S(1)} %select_bitcast_fusion.2), kind=kOutput, calls=%fused_computation.56 | convolution fusion | flops 537919488 | bytes 14680064 | tf_op jit(solution)/shard_map/tnk,nkj->tnj/dot_general | solution.py:28
  126.3 2.1 copy-done
  128.4 3.1 fusion.41
  131.4 8.3 %copy.112 = f32[32,256,256]{2,0,1:T(8,128)} copy(f32[32,256,256]{2,1,0:T(8,128)S(1)} %fusion.41) | data formatting | bytes 16777216 | tf_op jit(solution)/shard_map/tnk,tnj->nkj/dot_general | solution.py:36
  139.7 7.7 %gather_fusion.3 = f32[256,32,256]{2,1,0:T(8,128)} fusion(f32[32,256,256]{2,0,1:T(8,128)} %copy.112, s32[1024]{0:T(1024)S(1)} %pad_clamp_fusion), kind=kCustom, calls=%fused_computation.3.clone | custom fusion | bytes 16778240 | tf_op jit(solution)/shard_map/jit(_take)/gather | solution.py:66
  147.4 10.0 %copy.113 = f32[256,32,256]{0,2,1:T(8,128)} copy(f32[256,32,256]{2,1,0:T(8,128)} %gather_fusion.3) | data formatting | bytes 16777216 | tf_op jit(solution)/shard_map/jit(_take)/gather | solution.py:66
  157.4 4.0 %convolution_bitcast_fusion = f32[32,1,256,256]{2,3,0,1:T(8,128)S(1)} fusion(bf16[128,32,256]{0,2,1:T(8,128)(2,1)S(1)} %bitcast.86, f32[32,256,128]{2,1,0:T(8,128)} %copy-done), kind=kOutput, calls=%fused_computation.53 | convolution fusion | flops 546308096 | bytes 14680064 | tf_op jit(solution)/shard_map/tnk,tnj->nkj/dot_general | solution.py:36
  161.4 4.0 %select_bitcast_fusion = f32[32,1,256,256]{2,3,0,1:T(8,128)S(1)} fusion(f32[256,32,256]{0,2,1:T(8,128)} %copy.113, pred[256]{0:T(512)(128)(4,1)S(1)} %compare_and_fusion), kind=kLoop, calls=%fused_computation.8 | loop fusion | flops 2097152 | bytes 16777472 | tf_op jit(solution)/shard_map/stack | solution.py:70
  165.4 4.4 %fusion.1 = bf16[32,2,256,256]{2,3,0,1:T(8,128)(2,1)} fusion(f32[32,1,256,256]{2,3,0,1:T(8,128)S(1)} %select_bitcast_fusion, f32[32,1,256,256]{2,3,0,1:T(8,128)S(1)} %convolution_bitcast_fusion), kind=kLoop, calls=%fused_computation.7 | loop fusion | flops 12582912 | bytes 25165824 | tf_op jit(solution)/shard_map/convert_element_type | solution.py:84
  169.9 14.6 %copy.114 = bf16[32,2,256,256]{3,0,1,2:T(8,128)(2,1)} copy(bf16[32,2,256,256]{2,3,0,1:T(8,128)(2,1)} %fusion.1) | data formatting | bytes 16777216 | tf_op jit(solution)/shard_map/convert_element_type | solution.py:84
  184.8 2.5 slice_bitcast_fusion.1
  187.3 4.4 %copy.89 = bf16[32,256,256]{2,0,1:T(8,128)(2,1)} copy(bf16[32,256,256]{2,1,0:T(8,128)(2,1)S(1)} %slice_bitcast_fusion.1) | data formatting | bytes 8388608 | tf_op jit(solution)/shard_map/squeeze | solution.py:63
  191.6 5.0 %gather_fusion = bf16[256,32,256]{2,1,0:T(8,128)(2,1)} fusion(bf16[32,256,256]{2,0,1:T(8,128)(2,1)} %copy.89, s32[1024]{0:T(1024)S(1)} %pad_clamp_fusion.3), kind=kCustom, calls=%fused_computation.clone | custom fusion | bytes 8389632 | tf_op jit(solution)/shard_map/jit(_take)/gather | solution.py:63
  196.6 2.9 select_bitcast_fusion.3
  199.6 4.4 %fusion.26 = bf16[32,256,128]{2,1,0:T(8,128)(2,1)S(1)} fusion(bf16[128,32,256]{2,0,1:T(8,128)(2,1)} %collective-permute-done.1, bf16[32,256,256]{2,0,1:T(8,128)(2,1)S(1)} %select_bitcast_fusion.3), kind=kOutput, calls=%fused_computation.45 | convolution fusion | flops 536870912 | bytes 8388608 | tf_op jit(solution)/shard_map/tnj,nkj->tnk/dot_general | solution.py:32
  203.9 5.8 %fusion.5 = bf16[128,32,256]{0,2,1:T(8,128)(2,1)S(1)} fusion(f32[32,256,128]{2,1,0:T(8,128)S(1)} %copy-done.1, bf16[32,256,128]{2,1,0:T(8,128)(2,1)S(1)} %fusion.26, bf16[128,32,256]{0,2,1:T(8,128)(2,1)S(1)} %bitcast.87, bf16[32,2,256,256]{3,2,0,1:T(8,128)(2,1)} %all-gather.3.cloned.1.call-done), kind=kOutput, calls=%fused_computation.18 | convolution fusion | flops 562036736 | bytes 14680064 | tf_op jit(solution)/shard_map/tnj,nkj->tnk/dot_general | solution.py:32
  209.7 6.1 %convolution_bitcast_fusion.1 = f32[32,256,256]{1,2,0:T(8,128)} fusion(bf16[128,32,256]{0,2,1:T(8,128)(2,1)S(1)} %fusion.5, bf16[128,32,256]{0,2,1:T(8,128)(2,1)} %bitcast.10), kind=kOutput, calls=%fused_computation.54 | convolution fusion | flops 536870912 | bytes 12582912 | tf_op jit(solution)/shard_map/tnk,tnj->nkj/dot_general | solution.py:36
  215.8 10.3 %copy.107 = f32[32,256,256]{2,0,1:T(8,128)} copy(f32[32,256,256]{1,2,0:T(8,128)} %convolution_bitcast_fusion.1) | data formatting | bytes 16777216 | tf_op jit(solution)/shard_map/tnk,tnj->nkj/dot_general | solution.py:36
  226.2 7.8 %gather_fusion.2 = f32[256,32,256]{2,1,0:T(8,128)} fusion(f32[32,256,256]{2,0,1:T(8,128)} %copy.107, s32[1024]{0:T(1024)S(1)} %pad_clamp_fusion.1), kind=kCustom, calls=%fused_computation.1.clone | custom fusion | bytes 16778240 | tf_op jit(solution)/shard_map/jit(_take)/gather | solution.py:77
  234.0 10.0 %copy.108 = f32[256,32,256]{0,2,1:T(8,128)} copy(f32[256,32,256]{2,1,0:T(8,128)} %gather_fusion.2) | data formatting | bytes 16777216 | tf_op jit(solution)/shard_map/jit(_take)/gather | solution.py:77
  244.0 2.9 convolution_bitcast_fusion.2
  246.9 4.0 %select_bitcast_fusion.1 = f32[32,1,256,256]{2,3,0,1:T(8,128)S(1)} fusion(f32[256,32,256]{0,2,1:T(8,128)} %copy.108, pred[256]{0:T(512)(128)(4,1)S(1)} %compare_and_fusion.1), kind=kLoop, calls=%fused_computation.9 | loop fusion | flops 2097152 | bytes 16777472 | tf_op jit(solution)/shard_map/stack | solution.py:78
  250.9 4.5 %fusion = bf16[32,2,256,256]{2,3,0,1:T(8,128)(2,1)} fusion(f32[32,1,256,256]{2,3,0,1:T(8,128)S(1)} %select_bitcast_fusion.1, f32[32,1,256,256]{2,3,0,1:T(8,128)S(1)} %convolution_bitcast_fusion.2), kind=kLoop, calls=%fused_computation.5 | loop fusion | flops 12582912 | bytes 25165824 | tf_op jit(solution)/shard_map/convert_element_type | solution.py:81
  255.5 14.9 %copy.109 = bf16[32,2,256,256]{3,0,1,2:T(8,128)(2,1)} copy(bf16[32,2,256,256]{2,3,0,1:T(8,128)(2,1)} %fusion) | data formatting | bytes 16777216 | tf_op jit(solution)/shard_map/convert_element_type | solution.py:81
  270.3 6.2 %convert_bitcast_fusion = bf16[128,32,256]{2,0,1:T(8,128)(2,1)} fusion(bf16[128,32,256]{0,2,1:T(8,128)(2,1)S(1)} %fusion.5, bf16[32,256,256]{2,0,1:T(8,128)(2,1)} %copy-done.2), kind=kOutput, calls=%fused_computation.59 | convolution fusion | flops 537919488 | bytes 8388608 | tf_op jit(solution)/shard_map/tnj,nkj->tnk/dot_general | solution.py:32
  276.5 1.6 collective-permute-start.3
  278.1 1.4 fusion.44
  279.8 1.4 collective-permute-start.4
  281.3 43.4 %collective-permute-done.3 = bf16[128,32,256]{2,0,1:T(8,128)(2,1)} collective-permute-done((bf16[128,32,256]{2,0,1:T(8,128)(2,1)}, bf16[128,32,256]{2,0,1:T(8,128)(2,1)}, u32[]{:S(2)}, u32[]{:S(2)}) %collective-permute-start.3) | collective-permute-done | bytes 2097184 | tf_op jit(solution)/shard_map/ppermute | solution.py:13
  324.6 5.2 %fusion.20 = bf16[128,32,256]{2,0,1:T(8,128)(2,1)} fusion(bf16[128,32,256]{2,0,1:T(8,128)(2,1)} %collective-permute-done.3, bf16[128,32,256]{0,2,1:T(8,128)(2,1)S(1)} %fusion.5, bf16[32,1,256,256]{2,3,0,1:T(8,128)(2,1)} %copy.130), kind=kOutput, calls=%fused_computation.37 | convolution fusion | flops 540016640 | bytes 10485760 | tf_op jit(solution)/shard_map/tnj,nkj->tnk/dot_general | solution.py:32
  329.8 3.2 copy.104
  333.1 2.9 copy.117
  336.3 26.7 %reduce-scatter.3.cloned.1.call-done = bf16[32,2,32,256]{3,0,1,2:T(8,128)(2,1)} async-done(((bf16[32,2,256,256]{3,0,1,2:T(8,128)(2,1)}), bf16[32,2,32,256]{3,0,1,2:T(8,128)(2,1)}) %reduce-scatter.3.cloned.1.call-update) | async-done | bytes 1048592 | tf_op jit(solution)/shard_map/reduce_scatter | solution.py:80
  362.9 3.2 copy.118
  366.1 2.5 maximum_convert_fusion
  (50 shorter events, 5.7 us)
Async XLA Ops:
  7.2 20.5 %copy-start.6 = (bf16[128,8192]{1,0:T(8,128)(2,1)S(1)}, bf16[128,8192]{1,0:T(8,128)(2,1)}, u32[]{:S(2)}) copy-start(bf16[128,8192]{1,0:T(8,128)(2,1)} %param.9) | copy-start | bytes 6291460
  7.2 87.9 %all-gather.5.cloned.1.call-start = ((), (), s32[]{:S(2)}) async-start(), calls=%async_computation.3 | async-start | bytes 9437184 | tf_op jit(solution)/shard_map/all_gather | solution.py:50
  10.2 174.6 %all-gather.3.cloned.1.call-start = ((), (), s32[]{:S(2)}) async-start(), calls=%async_computation.2 | async-start | bytes 9437184 | tf_op jit(solution)/shard_map/all_gather | solution.py:61
  11.5 15.0 %collective-permute-start = (bf16[32,1,32,256]{3,2,0,1:T(8,128)(2,1)S(1)}, bf16[32,1,32,256]{3,2,0,1:T(8,128)(2,1)S(1)}, u32[]{:S(2)}, u32[]{:S(2)}) collective-permute-start(bf16[32,1,32,256]{3,2,0,1:T(8,128)(2,1)S(1)} %get-tuple-element.22), channel_id=1, source_target_pairs={{0,1},{1,0},{2,3},{3,2},{4,5},{5,4},{6,7},{7,6},{8,9},{9,8},{10,11... | collective-permute-start | bytes 1572872 | tf_op jit(solution)/shard_map/ppermute | solution.py:13
  27.6 250.5 %reduce-scatter.5.cloned.1.call-start = ((), (), s32[]{:S(2)}) async-start(), calls=%async_computation.5 | async-start | bytes 9437184 | tf_op jit(solution)/shard_map/reduce_scatter | solution.py:83
  30.1 9.4 %copy-start.8 = (s32[2,256]{1,0:T(2,128)S(1)}, s32[2,256]{1,0:T(2,128)}, u32[]{:S(2)}) copy-start(s32[2,256]{1,0:T(2,128)} %param.13) | copy-start | bytes 6148
  30.1 89.3 %collective-permute-start.2 = (bf16[128,8192]{0,1:T(8,128)(2,1)}, bf16[128,8192]{0,1:T(8,128)(2,1)}, u32[]{:S(2)}, u32[]{:S(2)}) collective-permute-start(bf16[128,8192]{0,1:T(8,128)(2,1)} %copy.96), channel_id=1, source_target_pairs={{0,2},{1,3},{2,0},{3,1},{4,6},{5,7},{6,4},{7,5},{8,10},{9,11},{10,... | collective-permute-start | bytes 6291464 | tf_op jit(solution)/shard_map/ppermute | solution.py:13
  35.2 122.3 %copy-start.4 = (bf16[128,8192]{0,1:T(8,128)(2,1)}, bf16[128,8192]{0,1:T(8,128)(2,1)S(1)}, u32[]{:S(2)}) copy-start(bf16[128,8192]{0,1:T(8,128)(2,1)S(1)} %copy.87) | copy-start | bytes 6291460
  38.1 88.2 %collective-permute-start.1 = (bf16[128,32,256]{2,0,1:T(8,128)(2,1)}, bf16[128,32,256]{2,0,1:T(8,128)(2,1)}, u32[]{:S(2)}, u32[]{:S(2)}) collective-permute-start(bf16[128,32,256]{2,0,1:T(8,128)(2,1)} %copy.90), channel_id=1, source_target_pairs={{0,1},{1,0},{2,3},{3,2},{4,5},{5,4},{6,7},{7,6},{8,9},{9,8},{10,11... | collective-permute-start | bytes 6291464 | tf_op jit(solution)/shard_map/ppermute | solution.py:13
  113.8 3.6 copy-start.3
  113.8 4.3 %copy-start.7 = (bf16[128,8192]{1,0:T(8,128)(2,1)S(1)}, bf16[128,8192]{1,0:T(8,128)(2,1)}, u32[]{:S(2)}) copy-start(bf16[128,8192]{1,0:T(8,128)(2,1)} %param.9) | copy-start | bytes 6291460
  117.3 2.1 copy-start.2
  126.3 2.1 copy-start
  184.5 178.4 %reduce-scatter.3.cloned.1.call-start = ((), (), s32[]{:S(2)}) async-start(), calls=%async_computation.4 | async-start | bytes 9437184 | tf_op jit(solution)/shard_map/reduce_scatter | solution.py:80
  199.5 4.4 %copy-start.1 = (f32[32,256,128]{2,1,0:T(8,128)S(1)}, f32[32,256,128]{2,1,0:T(8,128)}, u32[]{:S(2)}) copy-start(f32[32,256,128]{2,1,0:T(8,128)} %copy-done) | copy-start | bytes 12582916
  199.6 4.4 %copy-start.5 = (bf16[128,8192]{0,1:T(8,128)(2,1)S(1)}, bf16[128,8192]{0,1:T(8,128)(2,1)}, u32[]{:S(2)}) copy-start(bf16[128,8192]{0,1:T(8,128)(2,1)} %copy-done.4) | copy-start | bytes 6291460
  276.5 48.1 %collective-permute-start.3 = (bf16[128,32,256]{2,0,1:T(8,128)(2,1)}, bf16[128,32,256]{2,0,1:T(8,128)(2,1)}, u32[]{:S(2)}, u32[]{:S(2)}) collective-permute-start(bf16[128,32,256]{2,0,1:T(8,128)(2,1)} %convert_bitcast_fusion), channel_id=1, source_target_pairs={{0,2},{1,3},{2,0},{3,1},{4,6},{5,7},{6,4},{7,5},{8,10},{9,11},{10,... | collective-permute-start | bytes 6291464 | tf_op jit(solution)/shard_map/ppermute | solution.py:13
  279.8 86.3 %collective-permute-start.4 = (bf16[32,1,32,256]{3,2,1,0:T(8,128)(2,1)S(1)}, bf16[32,1,32,256]{3,2,1,0:T(8,128)(2,1)}, u32[]{:S(2)}, u32[]{:S(2)}) collective-permute-start(bf16[32,1,32,256]{3,2,1,0:T(8,128)(2,1)S(1)} %copy.115), channel_id=1, source_target_pairs={{0,1},{1,0},{2,3},{3,2},{4,5},{5,4},{6,7},{7,6},{8,9},{9,8},{10,11... | collective-permute-start | bytes 1572872 | tf_op jit(solution)/shard_map/ppermute | solution.py:13
Sparse Core Ops, SparseCore 0:
  10.3 84.7 all-gather.4
  96.7 80.5 all-gather.2
  184.6 88.0 reduce-scatter.4
  274.9 87.9 reduce-scatter.2
where the time goes:
time: 381 us; the launch traced here: 375 us
  local copies, waits for them, and re-layouts  141 us (37%)
  waiting for transfers between devices  137 us (36%)
  matrix products  45.7 us (12%)
  other arithmetic  27.3 us (7%)
  between operations  14.4 us (4%)
  starting transfers between devices  9.5 us (2%)
    all_gather x1, waiting for transfers between devices, shards(): first_full = lax.all_gather(first_weight, 'dp', axis=2, tiled=True)  55.3 us
    ppermute x5, waiting for transfers between devices, partner(): return lax.ppermute(value, axis, pairs)  55.3 us
    unnamed x25, local copies, waits for them, and re-layouts  26.7 us
    reduce_scatter x1, waiting for transfers between devices, shards(): lax.psum_scatter(first_term.astype(jnp.bfloat16), 'dp', scatter_dimension...  26.7 us
    dot_general x4, matrix products, contract_back(): jnp.einsum('tnj,nkj->tnk', left, right, preferred_element_type=jnp.float32)  21.5 us
    dot_general x2, local copies, waits for them, and re-layouts, outer_sum(): jnp.einsum('tnk,tnj->nkj', left, right, preferred_element_type=jnp.float32)  18.6 us
    gather x2, local copies, waits for them, and re-layouts, shards(): first_cross = jnp.take(outer_sum(partner_in, pre_grad), order_first, axis=1)  17.8 us
    gather x2, local copies, waits for them, and re-layouts, shards(): jnp.take(outer_sum(activated, cot_partner), order_second, axis=1)  17.7 us
  transfers between devices with their start and end apart: 9, of which 4 were waited for; matrix products, arithmetic and copies ran while one was open for 55% of the time, Pallas kernels for 0%

commit v1 on v0

--- a/solution.py
+++ b/solution.py
@@ -47,7 +47,7 @@
     order_second = orders[1]
     inverse_first = inverse_order(order_first)
     inverse_second = inverse_order(order_second)
-    first_full = lax.all_gather(first_weight, "dp", axis=2, tiled=True)
+    first_full = jnp.concatenate(lax.all_gather(first_weight, "dp"), axis=2)
     own_first = first_full[:, 0]
     cross_first = jnp.take(first_full[:, 1], inverse_first, axis=1)
     blocks_in = inputs.reshape(tok_rows, local_blocks, B)

time: 381 us -> 386 us (1.013)
  matrix products: 45.7 us -> 50.2 us
    reshape x0 -> x1, local copies, waits for them, and re-layouts: none -> 8.36 us  [shards(): first_full = jnp.concatenate(lax.all_gather(first_weight, 'dp'), axis=2)]
    unnamed x25 -> x22, local copies, waits for them, and re-layouts: 26.7 us -> 19.4 us
    squeeze x1 -> x0, local copies, waits for them, and re-layouts: 5.96 us -> none  [shards(): cross_first = jnp.take(first_full[:, 1], inverse_first, axis=1)]
    dot_general x2, matrix products: 8.13 us -> 12 us  [contract(): jnp.einsum('tnk,nkj->tnj', left, right, preferred_element_type=jnp.float32)]
  transfers between devices with their start and end apart: 9 -> 9, of which waited for: 4 -> 4; matrix products, arithmetic and copies ran while one was open for 55% -> 56% of each run, Pallas kernels for 0% -> 0%
where the time goes in v1:
time: 386 us; the launch traced here: 379 us
  local copies, waits for them, and re-layouts  139 us (36%)
  waiting for transfers between devices  139 us (36%)
  matrix products  50.2 us (13%)
  other arithmetic  26.9 us (7%)
  between operations  14.3 us (4%)
  starting transfers between devices  9.08 us (2%)
    all_gather x1, waiting for transfers between devices, shards(): first_full = jnp.concatenate(lax.all_gather(first_weight, 'dp'), axis=2)  57 us
    ppermute x5, waiting for transfers between devices, partner(): return lax.ppermute(value, axis, pairs)  55.3 us
    reduce_scatter x1, waiting for transfers between devices, shards(): lax.psum_scatter(first_term.astype(jnp.bfloat16), 'dp', scatter_dimension...  25.9 us
    dot_general x4, matrix products, contract_back(): jnp.einsum('tnj,nkj->tnk', left, right, preferred_element_type=jnp.float32)  22.1 us
    unnamed x22, local copies, waits for them, and re-layouts  19.4 us
    dot_general x2, local copies, waits for them, and re-layouts, outer_sum(): jnp.einsum('tnk,tnj->nkj', left, right, preferred_element_type=jnp.float32)  18.6 us
    gather x2, local copies, waits for them, and re-layouts, shards(): first_cross = jnp.take(outer_sum(partner_in, pre_grad), order_first, axis=1)  17.7 us
    gather x2, local copies, waits for them, and re-layouts, shards(): jnp.take(outer_sum(activated, cot_partner), order_second, axis=1)  17.7 us
  transfers between devices with their start and end apart: 9, of which 4 were waited for; matrix products, arithmetic and copies ran while one was open for 56% of the time, Pallas kernels for 0%

profile of v1, /device:TPU:0, one launch (start us, length us, event | category | flops | bytes accessed | tf_op | source)
XLA Modules:
  0.0 378.9 jit_solution(782064770786572341)
XLA Ops:
  9.2 3.0 collective-permute-start
  12.3 11.9 %collective-permute-done = bf16[32,1,32,256]{3,2,0,1:T(8,128)(2,1)S(1)} collective-permute-done((bf16[32,1,32,256]{3,2,0,1:T(8,128)(2,1)S(1)}, bf16[32,1,32,256]{3,2,0,1:T(8,128)(2,1)S(1)}, u32[]{:S(2)}, u32[]{:S(2)}) %collective-permute-start) | collective-permute-done | bytes 524320 | tf_op jit(solution)/shard_map/ppermute | solution.py:13
  25.4 2.4 copy.127
  27.8 1.8 collective-permute-start.2
  29.6 3.2 copy.118
  32.8 2.9 copy.121
  35.7 1.5 collective-permute-start.1
  37.4 57.0 %all-gather.6.cloned.1.call-done = bf16[256,2,32,256]{3,2,1,0:T(8,128)(2,1)} async-done(((bf16[32,2,32,256]{3,2,1,0:T(8,128)(2,1)}), bf16[256,2,32,256]{3,2,1,0:T(8,128)(2,1)}) %all-gather.6.cloned.1.call-update) | async-done | bytes 8388624 | tf_op jit(solution)/shard_map/all_gather | solution.py:50
  94.4 8.4 %copy.123 = bf16[32,2,8,32,256]{4,3,2,1,0:T(8,128)(2,1)} copy(bf16[32,2,8,32,256]{4,3,1,0,2:T(8,128)(2,1)} %bitcast.98) | data formatting | bytes 16777216 | tf_op jit(solution)/shard_map/reshape | solution.py:50
  102.7 3.1 slice.53
  105.9 4.4 %copy.183 = bf16[32,1,256,256]{3,0,2,1:T(8,128)(2,1)} copy(bf16[32,1,256,256]{3,2,1,0:T(8,128)(2,1)S(1)} %slice.53) | data formatting | bytes 8388608
  110.3 5.0 %gather_fusion.1 = bf16[256,32,256]{2,1,0:T(8,128)(2,1)} fusion(bf16[32,256,256]{2,0,1:T(8,128)(2,1)} %bitcast.97, s32[1024]{0:T(1024)S(1)} %pad_clamp_fusion.2), kind=kCustom, calls=%fused_computation.2.clone | custom fusion | bytes 8389632 | tf_op jit(solution)/shard_map/jit(_take)/gather | solution.py:52
  115.3 3.1 select_bitcast_fusion.2
  118.4 5.2 %fusion.25 = f32[32,256,128]{2,1,0:T(8,128)S(1)} fusion(bf16[32,2,256,256]{3,2,1,0:T(8,128)(2,1)} %bitcast.90, bf16[16,32,8,256]{3,2,1,0:T(8,128)(2,1)S(1)} %bitcast.96), kind=kOutput, calls=%fused_computation.47 | convolution fusion | flops 536870912 | bytes 10485760 | tf_op jit(solution)/shard_map/tnk,nkj->tnj/dot_general | solution.py:28
  123.5 6.9 %fusion.30 = f32[32,256,128]{2,1,0:T(8,128)S(1)} fusion(f32[32,256,128]{2,1,0:T(8,128)S(1)} %fusion.25, bf16[128,32,256]{0,2,1:T(8,128)(2,1)} %bitcast.13, bf16[32,256,256]{2,0,1:T(8,128)(2,1)S(1)} %select_bitcast_fusion.2), kind=kOutput, calls=%fused_computation.55 | convolution fusion | flops 537919488 | bytes 14680064 | tf_op jit(solution)/shard_map/tnk,nkj->tnj/dot_general | solution.py:28
  130.4 2.0 copy-done
  132.4 3.1 fusion.39
  135.5 8.3 %copy.143 = f32[32,256,256]{2,0,1:T(8,128)} copy(f32[32,256,256]{2,1,0:T(8,128)S(1)} %fusion.39) | data formatting | bytes 16777216 | tf_op jit(solution)/shard_map/tnk,tnj->nkj/dot_general | solution.py:36
  143.8 7.7 %gather_fusion.3 = f32[256,32,256]{2,1,0:T(8,128)} fusion(f32[32,256,256]{2,0,1:T(8,128)} %copy.143, s32[1024]{0:T(1024)S(1)} %pad_clamp_fusion), kind=kCustom, calls=%fused_computation.3.clone | custom fusion | bytes 16778240 | tf_op jit(solution)/shard_map/jit(_take)/gather | solution.py:66
  151.5 10.0 %copy.144 = f32[256,32,256]{0,2,1:T(8,128)} copy(f32[256,32,256]{2,1,0:T(8,128)} %gather_fusion.3) | data formatting | bytes 16777216 | tf_op jit(solution)/shard_map/jit(_take)/gather | solution.py:66
  161.5 4.0 %convolution_bitcast_fusion = f32[32,1,256,256]{2,3,0,1:T(8,128)S(1)} fusion(bf16[128,32,256]{0,2,1:T(8,128)(2,1)S(1)} %bitcast.93, f32[32,256,128]{2,1,0:T(8,128)} %copy-done), kind=kOutput, calls=%fused_computation.52 | convolution fusion | flops 546308096 | bytes 14680064 | tf_op jit(solution)/shard_map/tnk,tnj->nkj/dot_general | solution.py:36
  165.5 4.0 %select_bitcast_fusion = f32[32,1,256,256]{2,3,0,1:T(8,128)S(1)} fusion(f32[256,32,256]{0,2,1:T(8,128)} %copy.144, pred[256]{0:T(512)(128)(4,1)S(1)} %compare_and_fusion), kind=kLoop, calls=%fused_computation.8 | loop fusion | flops 2097152 | bytes 16777472 | tf_op jit(solution)/shard_map/stack | solution.py:70
  169.5 4.4 %fusion.1 = bf16[32,2,256,256]{2,3,0,1:T(8,128)(2,1)} fusion(f32[32,1,256,256]{2,3,0,1:T(8,128)S(1)} %select_bitcast_fusion, f32[32,1,256,256]{2,3,0,1:T(8,128)S(1)} %convolution_bitcast_fusion), kind=kLoop, calls=%fused_computation.7 | loop fusion | flops 12582912 | bytes 25165824 | tf_op jit(solution)/shard_map/convert_element_type | solution.py:84
  173.9 14.6 %copy.145 = bf16[32,2,256,256]{3,0,1,2:T(8,128)(2,1)} copy(bf16[32,2,256,256]{2,3,0,1:T(8,128)(2,1)} %fusion.1) | data formatting | bytes 16777216 | tf_op jit(solution)/shard_map/convert_element_type | solution.py:84
  188.8 2.5 slice_bitcast_fusion.1
  191.3 4.4 %copy.120 = bf16[32,256,256]{2,0,1:T(8,128)(2,1)} copy(bf16[32,256,256]{2,1,0:T(8,128)(2,1)S(1)} %slice_bitcast_fusion.1) | data formatting | bytes 8388608 | tf_op jit(solution)/shard_map/squeeze | solution.py:63
  195.7 5.0 %gather_fusion = bf16[256,32,256]{2,1,0:T(8,128)(2,1)} fusion(bf16[32,256,256]{2,0,1:T(8,128)(2,1)} %copy.120, s32[1024]{0:T(1024)S(1)} %pad_clamp_fusion.3), kind=kCustom, calls=%fused_computation.clone | custom fusion | bytes 8389632 | tf_op jit(solution)/shard_map/jit(_take)/gather | solution.py:63
  200.7 3.1 select_bitcast_fusion.3
  203.8 4.4 %fusion.22 = bf16[32,256,128]{2,1,0:T(8,128)(2,1)S(1)} fusion(bf16[128,32,256]{2,0,1:T(8,128)(2,1)} %collective-permute-done.1, bf16[32,256,256]{2,0,1:T(8,128)(2,1)S(1)} %select_bitcast_fusion.3), kind=kOutput, calls=%fused_computation.42 | convolution fusion | flops 536870912 | bytes 8388608 | tf_op jit(solution)/shard_map/tnj,nkj->tnk/dot_general | solution.py:32
  208.2 5.8 %fusion.5 = bf16[128,32,256]{0,2,1:T(8,128)(2,1)S(1)} fusion(f32[32,256,128]{2,1,0:T(8,128)S(1)} %copy-done.1, bf16[32,256,128]{2,1,0:T(8,128)(2,1)S(1)} %fusion.22, bf16[128,32,256]{0,2,1:T(8,128)(2,1)S(1)} %bitcast.94, bf16[32,2,256,256]{3,2,0,1:T(8,128)(2,1)} %all-gather.4.cloned.1.call-done), kind=kOutput, calls=%fused_computation.18 | convolution fusion | flops 562036736 | bytes 14680064 | tf_op jit(solution)/shard_map/tnj,nkj->tnk/dot_general | solution.py:32
  213.9 6.1 %convolution_bitcast_fusion.1 = f32[32,256,256]{1,2,0:T(8,128)} fusion(bf16[128,32,256]{0,2,1:T(8,128)(2,1)S(1)} %fusion.5, bf16[128,32,256]{0,2,1:T(8,128)(2,1)} %bitcast.13), kind=kOutput, calls=%fused_computation.53 | convolution fusion | flops 536870912 | bytes 12582912 | tf_op jit(solution)/shard_map/tnk,tnj->nkj/dot_general | solution.py:36
  220.1 10.3 %copy.138 = f32[32,256,256]{2,0,1:T(8,128)} copy(f32[32,256,256]{1,2,0:T(8,128)} %convolution_bitcast_fusion.1) | data formatting | bytes 16777216 | tf_op jit(solution)/shard_map/tnk,tnj->nkj/dot_general | solution.py:36
  230.4 7.8 %gather_fusion.2 = f32[256,32,256]{2,1,0:T(8,128)} fusion(f32[32,256,256]{2,0,1:T(8,128)} %copy.138, s32[1024]{0:T(1024)S(1)} %pad_clamp_fusion.1), kind=kCustom, calls=%fused_computation.1.clone | custom fusion | bytes 16778240 | tf_op jit(solution)/shard_map/jit(_take)/gather | solution.py:77
  238.2 9.9 %copy.139 = f32[256,32,256]{0,2,1:T(8,128)} copy(f32[256,32,256]{2,1,0:T(8,128)} %gather_fusion.2) | data formatting | bytes 16777216 | tf_op jit(solution)/shard_map/jit(_take)/gather | solution.py:77
  248.1 2.8 convolution_bitcast_fusion.2
  251.0 4.0 %select_bitcast_fusion.1 = f32[32,1,256,256]{2,3,0,1:T(8,128)S(1)} fusion(f32[256,32,256]{0,2,1:T(8,128)} %copy.139, pred[256]{0:T(512)(128)(4,1)S(1)} %compare_and_fusion.1), kind=kLoop, calls=%fused_computation.9 | loop fusion | flops 2097152 | bytes 16777472 | tf_op jit(solution)/shard_map/stack | solution.py:78
  255.0 4.4 %fusion = bf16[32,2,256,256]{2,3,0,1:T(8,128)(2,1)} fusion(f32[32,1,256,256]{2,3,0,1:T(8,128)S(1)} %select_bitcast_fusion.1, f32[32,1,256,256]{2,3,0,1:T(8,128)S(1)} %convolution_bitcast_fusion.2), kind=kLoop, calls=%fused_computation.5 | loop fusion | flops 12582912 | bytes 25165824 | tf_op jit(solution)/shard_map/convert_element_type | solution.py:81
  259.4 14.9 %copy.140 = bf16[32,2,256,256]{3,0,1,2:T(8,128)(2,1)} copy(bf16[32,2,256,256]{2,3,0,1:T(8,128)(2,1)} %fusion) | data formatting | bytes 16777216 | tf_op jit(solution)/shard_map/convert_element_type | solution.py:81
  274.3 6.2 %convert_bitcast_fusion = bf16[128,32,256]{2,0,1:T(8,128)(2,1)} fusion(bf16[128,32,256]{0,2,1:T(8,128)(2,1)S(1)} %fusion.5, bf16[32,256,256]{2,0,1:T(8,128)(2,1)} %copy-done.2), kind=kOutput, calls=%fused_computation.58 | convolution fusion | flops 537919488 | bytes 8388608 | tf_op jit(solution)/shard_map/tnj,nkj->tnk/dot_general | solution.py:32
  280.5 1.3 collective-permute-start.3
  281.9 1.5 fusion.42
  285.0 43.4 %collective-permute-done.3 = bf16[128,32,256]{2,0,1:T(8,128)(2,1)} collective-permute-done((bf16[128,32,256]{2,0,1:T(8,128)(2,1)}, bf16[128,32,256]{2,0,1:T(8,128)(2,1)}, u32[]{:S(2)}, u32[]{:S(2)}) %collective-permute-start.3) | collective-permute-done | bytes 2097184 | tf_op jit(solution)/shard_map/ppermute | solution.py:13
  328.4 5.8 %fusion.20 = bf16[128,32,256]{2,0,1:T(8,128)(2,1)} fusion(bf16[128,32,256]{2,0,1:T(8,128)(2,1)} %collective-permute-done.3, bf16[128,32,256]{0,2,1:T(8,128)(2,1)S(1)} %fusion.5, bf16[32,2,256,256]{3,2,1,0:T(8,128)(2,1)} %bitcast.91), kind=kOutput, calls=%fused_computation.38 | convolution fusion | flops 540016640 | bytes 10485760 | tf_op jit(solution)/shard_map/tnj,nkj->tnk/dot_general | solution.py:32
  334.2 3.2 copy.135
  337.4 2.9 copy.148
  340.6 25.9 %reduce-scatter.3.cloned.1.call-done = bf16[32,2,32,256]{3,0,1,2:T(8,128)(2,1)} async-done(((bf16[32,2,256,256]{3,0,1,2:T(8,128)(2,1)}), bf16[32,2,32,256]{3,0,1,2:T(8,128)(2,1)}) %reduce-scatter.3.cloned.1.call-update) | async-done | bytes 1048592 | tf_op jit(solution)/shard_map/reduce_scatter | solution.py:80
  366.5 3.2 copy.149
  369.6 2.5 maximum_convert_fusion
  (48 shorter events, 5.5 us)
Async XLA Ops:
  7.2 18.2 %copy-start.5 = (bf16[128,8192]{1,0:T(8,128)(2,1)S(1)}, bf16[128,8192]{1,0:T(8,128)(2,1)}, u32[]{:S(2)}) copy-start(bf16[128,8192]{1,0:T(8,128)(2,1)} %param.9) | copy-start | bytes 6291460
  7.2 87.2 %all-gather.6.cloned.1.call-start = ((), (), s32[]{:S(2)}) async-start(), calls=%async_computation.5 | async-start | bytes 9437184 | tf_op jit(solution)/shard_map/all_gather | solution.py:50
  7.9 180.9 %all-gather.4.cloned.1.call-start = ((), (), s32[]{:S(2)}) async-start(), calls=%async_computation.2 | async-start | bytes 9437184 | tf_op jit(solution)/shard_map/all_gather | solution.py:61
  9.2 15.0 %collective-permute-start = (bf16[32,1,32,256]{3,2,0,1:T(8,128)(2,1)S(1)}, bf16[32,1,32,256]{3,2,0,1:T(8,128)(2,1)S(1)}, u32[]{:S(2)}, u32[]{:S(2)}) collective-permute-start(bf16[32,1,32,256]{3,2,0,1:T(8,128)(2,1)S(1)} %get-tuple-element.23), channel_id=1, source_target_pairs={{0,1},{1,0},{2,3},{3,2},{4,5},{5,4},{6,7},{7,6},{8,9},{9,8},{10,11... | collective-permute-start | bytes 1572872 | tf_op jit(solution)/shard_map/ppermute | solution.py:13
  25.3 256.6 %reduce-scatter.5.cloned.1.call-start = ((), (), s32[]{:S(2)}) async-start(), calls=%async_computation.4 | async-start | bytes 9437184 | tf_op jit(solution)/shard_map/reduce_scatter | solution.py:83
  27.8 9.4 %copy-start.7 = (s32[2,256]{1,0:T(2,128)S(1)}, s32[2,256]{1,0:T(2,128)}, u32[]{:S(2)}) copy-start(s32[2,256]{1,0:T(2,128)} %param.13) | copy-start | bytes 6148
  27.8 95.7 %collective-permute-start.2 = (bf16[128,8192]{0,1:T(8,128)(2,1)}, bf16[128,8192]{0,1:T(8,128)(2,1)}, u32[]{:S(2)}, u32[]{:S(2)}) collective-permute-start(bf16[128,8192]{0,1:T(8,128)(2,1)} %copy.127), channel_id=1, source_target_pairs={{0,2},{1,3},{2,0},{3,1},{4,6},{5,7},{6,4},{7,5},{8,10},{9,11},{10,... | collective-permute-start | bytes 6291464 | tf_op jit(solution)/shard_map/ppermute | solution.py:13
  32.8 128.7 %copy-start.3 = (bf16[128,8192]{0,1:T(8,128)(2,1)}, bf16[128,8192]{0,1:T(8,128)(2,1)S(1)}, u32[]{:S(2)}) copy-start(bf16[128,8192]{0,1:T(8,128)(2,1)S(1)} %copy.118) | copy-start | bytes 6291460
  35.7 94.7 %collective-permute-start.1 = (bf16[128,32,256]{2,0,1:T(8,128)(2,1)}, bf16[128,32,256]{2,0,1:T(8,128)(2,1)}, u32[]{:S(2)}, u32[]{:S(2)}) collective-permute-start(bf16[128,32,256]{2,0,1:T(8,128)(2,1)} %copy.121), channel_id=1, source_target_pairs={{0,1},{1,0},{2,3},{3,2},{4,5},{5,4},{6,7},{7,6},{8,9},{9,8},{10,11... | collective-permute-start | bytes 6291464 | tf_op jit(solution)/shard_map/ppermute | solution.py:13
  115.3 3.1 copy-start.6
  118.3 5.2 %copy-start.2 = (bf16[32,256,256]{2,0,1:T(8,128)(2,1)}, bf16[32,256,256]{2,0,1:T(8,128)(2,1)S(1)}, u32[]{:S(2)}) copy-start(bf16[32,256,256]{2,0,1:T(8,128)(2,1)S(1)} %select_bitcast_fusion.2) | copy-start | bytes 12582916
  130.4 2.0 copy-start
  188.6 177.9 %reduce-scatter.3.cloned.1.call-start = ((), (), s32[]{:S(2)}) async-start(), calls=%async_computation.3 | async-start | bytes 9437184 | tf_op jit(solution)/shard_map/reduce_scatter | solution.py:80
  203.8 4.4 %copy-start.1 = (f32[32,256,128]{2,1,0:T(8,128)S(1)}, f32[32,256,128]{2,1,0:T(8,128)}, u32[]{:S(2)}) copy-start(f32[32,256,128]{2,1,0:T(8,128)} %copy-done) | copy-start | bytes 12582916
  203.8 4.4 %copy-start.4 = (bf16[128,8192]{0,1:T(8,128)(2,1)S(1)}, bf16[128,8192]{0,1:T(8,128)(2,1)}, u32[]{:S(2)}) copy-start(bf16[128,8192]{0,1:T(8,128)(2,1)} %copy-done.3) | copy-start | bytes 6291460
  280.5 47.8 %collective-permute-start.3 = (bf16[128,32,256]{2,0,1:T(8,128)(2,1)}, bf16[128,32,256]{2,0,1:T(8,128)(2,1)}, u32[]{:S(2)}, u32[]{:S(2)}) collective-permute-start(bf16[128,32,256]{2,0,1:T(8,128)(2,1)} %convert_bitcast_fusion), channel_id=1, source_target_pairs={{0,2},{1,3},{2,0},{3,1},{4,6},{5,7},{6,4},{7,5},{8,10},{9,11},{10,... | collective-permute-start | bytes 6291464 | tf_op jit(solution)/shard_map/ppermute | solution.py:13
  283.7 85.9 %collective-permute-start.4 = (bf16[32,1,32,256]{3,2,1,0:T(8,128)(2,1)S(1)}, bf16[32,1,32,256]{3,2,1,0:T(8,128)(2,1)}, u32[]{:S(2)}, u32[]{:S(2)}) collective-permute-start(bf16[32,1,32,256]{3,2,1,0:T(8,128)(2,1)S(1)} %copy.146), channel_id=1, source_target_pairs={{0,1},{1,0},{2,3},{3,2},{4,5},{5,4},{6,7},{7,6},{8,9},{9,8},{10,11... | collective-permute-start | bytes 1572872 | tf_op jit(solution)/shard_map/ppermute | solution.py:13
Sparse Core Ops, SparseCore 0:
  9.6 84.7 all-gather.5
  96.0 80.5 all-gather.3
  188.7 87.5 reduce-scatter.4
  278.5 87.9 reduce-scatter.2
